TPU v7x, 256 devices: a whole 4x4x8 slice. The times are simulated.
256 devices in a mesh: sect: 4 (over y), pass: 16 (over z, core), qry: 4 (over x).
Axes of the slice: x: 4, y: 4, z: 8, core: 2. Of those that a mesh axis runs over, the one named last changes fastest.
Arguments:
- query_emb: bfloat16 [8192, 4096], P(('sect', 'qry')), may hold values from -0.2 to 0.2
- passage_emb: bfloat16 [16384, 4096], P(('sect', 'pass')), may hold values from -0.2 to 0.2
- block_ids: int32 [32, 64], P(('sect', 'qry')), may hold values from 0 to 255, as said below
- positives: int32 [8192], P(('sect', 'qry')), may hold values from 0 to 16383, as said below
Outputs:
- query_grad: bfloat16 [8192, 4096], P(('sect', 'qry'), 'pass')
- pool_grad: bfloat16 [16384, 4096], P(('sect', 'pass', 'qry'))
Inputs may be any that keep to these rules, and one draw needn't show every extreme that they name: `block_ids`: each row names 64 different passage blocks. `positives`: the positive passage of a query lies in a block that its query block's row of block_ids names.
All inputs are finite; a program needn't handle non-finite values.
Results may differ from a plain program's by a relative error of at most 0.015.
Values may be sent and summed in bfloat16 or wider, within the bound.
A program may use at most 128 MiB of HBM per device.

v0:
```python
import jax
import jax.numpy as jnp
from jax import lax
from jax.sharding import PartitionSpec as P

QBR = 256
PBR = 64
LOGIT_SCALE = 50.0
NEG_FILL = -1e30


def inner_rows(first_operand, second_operand):
    return lax.dot_general(
        first_operand, second_operand, (((1,), (1,)), ((), ())), preferred_element_type=jnp.float32
    )


def inner_cols(first_operand, second_operand):
    return lax.dot_general(
        first_operand, second_operand, (((0,), (0,)), ((), ())), preferred_element_type=jnp.float32
    )


def body(query_emb, passage_emb, block_ids, positives):
    section_count = lax.axis_size("sect")
    shard_count = lax.axis_size("pass")
    shard_index = lax.axis_index("pass")
    query_rows, embed_width = query_emb.shape
    passage_rows = passage_emb.shape[0]
    query_blocks = query_rows // QBR
    per_piece = passage_rows // PBR
    local_count = section_count * per_piece
    candidates = section_count * passage_rows
    gathered = lax.all_gather(passage_emb, "sect", axis=0, tiled=True)
    local_ids = jnp.arange(local_count, dtype=jnp.int32)
    global_blocks = (
        local_ids // per_piece * shard_count + shard_index
    ) * per_piece + local_ids % per_piece
    allowed = jnp.any(block_ids[:, :, None] == global_blocks[None, None, :], axis=1)
    allowed_rows = jnp.broadcast_to(
        allowed[:, None, :, None], (query_blocks, QBR, local_count, PBR)
    )
    allowed_rows = allowed_rows.reshape(query_rows, candidates)
    global_rows = (
        global_blocks[:, None] * PBR + jnp.arange(PBR, dtype=jnp.int32)[None, :]
    ).reshape(candidates)
    target = (positives[:, None] == global_rows[None, :]).astype(jnp.float32)
    scores = LOGIT_SCALE * inner_rows(query_emb, gathered)
    local_top = jnp.max(jnp.where(allowed_rows, scores, NEG_FILL), axis=1)
    row_top = lax.pmax(local_top, "pass")
    exp_terms = jnp.where(allowed_rows, jnp.exp(scores - row_top[:, None]), 0.0)
    row_sum = lax.psum(jnp.sum(exp_terms, axis=1), "pass")
    score_grad = (LOGIT_SCALE * (exp_terms / row_sum[:, None] - target)).astype(jnp.bfloat16)
    query_part = jnp.dot(score_grad, gathered, preferred_element_type=jnp.float32)
    pool_part = inner_cols(score_grad, query_emb)
    query_part = query_part.astype(jnp.bfloat16)
    pool_part = pool_part.astype(jnp.bfloat16)
    query_grad = (
        lax.psum_scatter(query_part, "pass", scatter_dimension=1, tiled=True)
        .astype(jnp.float32)
        .astype(jnp.bfloat16)
    )
    pool_grad = (
        lax.psum_scatter(pool_part, ("sect", "qry"), scatter_dimension=0, tiled=True)
        .astype(jnp.float32)
        .astype(jnp.bfloat16)
    )
    return (query_grad, pool_grad)


def solution(mesh):
    return jax.shard_map(
        body,
        mesh=mesh,
        in_specs=(
            P(("sect", "qry"), None),
            P(("sect", "pass"), None),
            P(("sect", "qry"), None),
            P(("sect", "qry")),
        ),
        out_specs=(P(("sect", "qry"), "pass"), P(("sect", "pass", "qry"), None)),
        check_vma=False,
    )
```

profile of v0, /device:TPU:2, one launch (start us, length us, event | category | flops | bytes accessed | tf_op | source)
XLA Modules:
  0.0 329.6 jit_solution(13325460295013534195)
XLA Ops:
  7.2 0.0 copy-start
  7.2 0.0 all-gather.2.cloned.1.call-start
  7.2 0.7 all-gather.2.cloned.1.call-update
  7.9 0.0 reduce-scatter.3.cloned.1.call-start
  8.0 0.1 iota_add_fusion
  8.0 0.1 add.81
  8.1 0.0 copy-done
  8.1 0.2 compare_reduce_fusion
  8.3 0.3 broadcast_in_dim.8
  8.7 2.4 reshape.76
  11.1 87.4 %all-gather.2.cloned.1.call-done = bf16[1024,4096]{1,0:T(8,128)(2,1)} async-done(((bf16[256,4096]{1,0:T(8,128)(2,1)}), bf16[1024,4096]{1,0:T(8,128)(2,1)}) %all-gather.2.cloned.1.call-update) | async-done | bytes 8388624 | tf_op jit(solution)/shard_map/all_gather | solution.py:34
  98.4 8.4 %select_reduce_fusion = (f32[512]{0:T(512)S(1)}, f32[512,1024]{1,0:T(8,128)S(1)}) fusion(pred[512,1024]{1,0:T(32,128)(4,1)S(1)} %reshape.76, bf16[512,4096]{1,0:T(8,128)(2,1)} %param.4, bf16[1024,4096]{1,0:T(8,128)(2,1)} %all-gather.2.cloned.1.call-done), kind=kOutput, calls=%fused_computation.4 | convolution fusion | flops 4296539648 | bytes 15206400 | tf_op jit(solution)/shard_map/dot_general | solution.py:13
  106.8 0.0 copy-start.1
  106.9 26.1 %pmax.7 = f32[512]{0:T(512)S(1)} all-reduce(f32[512]{0:T(512)S(1)} %get-tuple-element.2), channel_id=1, replica_groups=mesh['sect'=4,'pass'=16,'qry'=4] {'pass'}, use_global_device_ids=true, to_apply=%region_2.3 | all-reduce | flops 512 | bytes 4096 | tf_op jit(solution)/shard_map/pmax | solution.py:50
  133.0 0.7 fusion
  133.7 23.5 %psum.7 = f32[512]{0:T(512)S(1)} all-reduce(f32[512]{0:T(512)S(1)} %fusion), channel_id=1, replica_groups=mesh['sect'=4,'pass'=16,'qry'=4] {'pass'}, use_global_device_ids=true, to_apply=%region_4.5 | all-reduce | flops 512 | bytes 4096 | tf_op jit(solution)/shard_map/psum | solution.py:52
  157.2 0.0 copy-done.1
  157.2 10.3 %convolution_convert_fusion.1 = bf16[512,4096]{1,0:T(8,128)(2,1)} fusion(bf16[1024,4096]{1,0:T(8,128)(2,1)} %all-gather.2.cloned.1.call-done, pred[512,1024]{1,0:T(32,128)(4,1)S(1)} %reshape.76, f32[512,1024]{1,0:T(8,128)S(1)} %get-tuple-element.3, s32[1024]{0:T(1024)S(1)} %add.81, f32[512]{0:T(512)S(1)} %psum.7, f32[512]{0:T(512)S(1)} %pmax.7, ...), kind=kOutput, calls=%fused_computation.1 | convolution fusion | flops 4301783040 | bytes 15214592 | tf_op jit(solution)/shard_map/dot_general | solution.py:54
  167.5 0.0 reduce-scatter.3.cloned.1.call-update
  167.5 0.0 reduce-scatter.5.cloned.1.call-start
  167.6 9.5 %convolution_convert_fusion = bf16[1024,4096]{1,0:T(8,128)(2,1)} fusion(bf16[512,4096]{1,0:T(8,128)(2,1)} %param.4, pred[512,1024]{1,0:T(32,128)(4,1)S(1)} %reshape.76, f32[512,1024]{1,0:T(8,128)S(1)} %get-tuple-element.3, s32[1024]{0:T(1024)S(1)} %add.81, f32[512]{0:T(512)S(1)} %psum.7, f32[512]{0:T(512)S(1)} %pmax.7, s32[512]{0:T(512)S(1)} %copy-done.1), kind=kOutput, calls=%fused_computation | convolution fusion | flops 4303880192 | bytes 15214592 | tf_op jit(solution)/shard_map/dot_general | solution.py:19
  177.1 0.0 reduce-scatter.5.cloned.1.call-update
  177.1 52.2 %reduce-scatter.3.cloned.1.call-done = bf16[512,256]{1,0:T(8,128)(2,1)} async-done(((bf16[512,4096]{1,0:T(8,128)(2,1)}), bf16[512,256]{1,0:T(8,128)(2,1)}) %reduce-scatter.3.cloned.1.call-update) | async-done | bytes 262160 | tf_op jit(solution)/shard_map/reduce_scatter | solution.py:59
  229.3 93.7 %reduce-scatter.5.cloned.1.call-done = bf16[64,4096]{1,0:T(8,128)(2,1)} async-done(((bf16[1024,4096]{1,0:T(8,128)(2,1)}), bf16[64,4096]{1,0:T(8,128)(2,1)}) %reduce-scatter.5.cloned.1.call-update) | async-done | bytes 524304 | tf_op jit(solution)/shard_map/reduce_scatter | solution.py:64
  (1 shorter events, 0.0 us)
Async XLA Ops:
  7.2 1.0 copy-start
  7.2 91.2 %all-gather.2.cloned.1.call-start = ((), (), s32[]{:S(2)}) async-start(), calls=%async_computation.2 | async-start | bytes 10485760 | tf_op jit(solution)/shard_map/all_gather | solution.py:34
  7.9 221.4 %reduce-scatter.3.cloned.1.call-start = ((), (), s32[]{:S(2)}) async-start(), calls=%async_computation.3 | async-start | bytes 4456448 | tf_op jit(solution)/shard_map/reduce_scatter | solution.py:59
  106.8 50.4 %copy-start.1 = (s32[512]{0:T(512)S(1)}, s32[512]{0:T(512)}, u32[]{:S(2)}) copy-start(s32[512]{0:T(512)} %param.7) | copy-start | bytes 6148
  167.5 155.5 %reduce-scatter.5.cloned.1.call-start = ((), (), s32[]{:S(2)}) async-start(), calls=%async_computation.4 | async-start | bytes 8912896 | tf_op jit(solution)/shard_map/reduce_scatter | solution.py:64
Sparse Core Ops, SparseCore 0:
  9.8 88.5 all-gather.1
  167.6 61.6 reduce-scatter.2
  233.6 89.3 reduce-scatter.4
where the time goes:
time: 330 us
  waiting for transfers between devices  234 us (71%)
  blocking collectives  49.7 us (15%)
  matrix products  28.2 us (9%)
  between operations  13.8 us (4%)
    reduce_scatter x1, waiting for transfers between devices, body(): lax.psum_scatter(pool_part, ('sect', 'qry'), scatter_dimension=0, tiled=T...  93.7 us
    all_gather x1, waiting for transfers between devices, body(): gathered = lax.all_gather(passage_emb, 'sect', axis=0, tiled=True)  87.4 us
    reduce_scatter x1, waiting for transfers between devices, body(): lax.psum_scatter(query_part, 'pass', scatter_dimension=1, tiled=True)  52.2 us
    pmax x1, blocking collectives, body(): row_top = lax.pmax(local_top, 'pass')  26.1 us
    psum x1, blocking collectives, body(): row_sum = lax.psum(jnp.sum(exp_terms, axis=1), 'pass')  23.5 us
    dot_general x1, matrix products, body(): jnp.dot(score_grad, gathered, preferred_element_type=jnp.float32)  10.3 us
    dot_general x1, matrix products, inner_cols(): lax.dot_general(first_operand, second_operand, (((0,), (0,)), ((), ())),...  9.5 us
    dot_general x1, matrix products, inner_rows(): lax.dot_general(first_operand, second_operand, (((1,), (1,)), ((), ())),...  8.42 us
  transfers between devices with their start and end apart: 3, of which 3 were waited for; matrix products, arithmetic and copies ran while one was open for 4% of the time, Pallas kernels for 0%

commit v1 on v0

--- a/solution.py
+++ b/solution.py
@@ -7,6 +7,11 @@
 PBR = 64
 LOGIT_SCALE = 50.0
 NEG_FILL = -1e30
+
+
+def gather_over(array, axis, dim):
+    sent = jnp.stack([array] * lax.axis_size(axis))
+    return jnp.concatenate(lax.all_to_all(sent, axis, 0, 0), axis=dim)
 
 
 def inner_rows(first_operand, second_operand):
@@ -31,7 +36,7 @@
     per_piece = passage_rows // PBR
     local_count = section_count * per_piece
     candidates = section_count * passage_rows
-    gathered = lax.all_gather(passage_emb, "sect", axis=0, tiled=True)
+    gathered = gather_over(passage_emb, "sect", 0)
     local_ids = jnp.arange(local_count, dtype=jnp.int32)
     global_blocks = (
         local_ids // per_piece * shard_count + shard_index

time: 330 us -> 344 us (1.042)
  local copies, waits for them, and re-layouts: 2.82 us -> 8.67 us
  starting transfers between devices: 0.12 us -> 5.87 us
    all_to_all x0 -> x1, waiting for transfers between devices: none -> 90.9 us  [gather_over(): return jnp.concatenate(lax.all_to_all(sent, axis, 0, 0), axis=dim)]
    all_gather x1 -> x0, waiting for transfers between devices: 87.4 us -> none  [body(): gathered = lax.all_gather(passage_emb, 'sect', axis=0, tiled=True)]
    another operation x0 -> x1, local copies, waits for them, and re-layouts: none -> 5.86 us  [gather_over(): sent = jnp.stack([array] * lax.axis_size(axis))]
    all_to_all x0 -> x1, starting transfers between devices: none -> 5.78 us  [gather_over(): return jnp.concatenate(lax.all_to_all(sent, axis, 0, 0), axis=dim)]
where the time goes in v1:
time: 344 us
  waiting for transfers between devices  235 us (68%)
  blocking collectives  51.5 us (15%)
  matrix products  28.2 us (8%)
  between operations  14.1 us (4%)
  local copies, waits for them, and re-layouts  8.67 us (3%)
  starting transfers between devices  5.87 us (2%)
    reduce_scatter x1, waiting for transfers between devices, body(): lax.psum_scatter(pool_part, ('sect', 'qry'), scatter_dimension=0, tiled=T...  93.6 us
    all_to_all x1, waiting for transfers between devices, gather_over(): return jnp.concatenate(lax.all_to_all(sent, axis, 0, 0), axis=dim)  90.9 us
    reduce_scatter x1, waiting for transfers between devices, body(): lax.psum_scatter(query_part, 'pass', scatter_dimension=1, tiled=True)  50.3 us
    pmax x1, blocking collectives, body(): row_top = lax.pmax(local_top, 'pass')  28 us
    psum x1, blocking collectives, body(): row_sum = lax.psum(jnp.sum(exp_terms, axis=1), 'pass')  23.5 us
    dot_general x1, matrix products, body(): jnp.dot(score_grad, gathered, preferred_element_type=jnp.float32)  10.3 us
    dot_general x1, matrix products, inner_cols(): lax.dot_general(first_operand, second_operand, (((0,), (0,)), ((), ())),...  9.49 us
    dot_general x1, matrix products, inner_rows(): lax.dot_general(first_operand, second_operand, (((1,), (1,)), ((), ())),...  8.42 us
  transfers between devices with their start and end apart: 3, of which 3 were waited for; matrix products, arithmetic and copies ran while one was open for 4% of the time, Pallas kernels for 0%

profile of v1, /device:TPU:2, one launch (start us, length us, event | category | flops | bytes accessed | tf_op | source)
XLA Modules:
  0.0 344.2 jit_solution(7399749634560542439)
XLA Ops:
  7.2 5.9 %stack.2 = bf16[4,256,4096]{2,1,0:T(8,128)(2,1)} broadcast(bf16[256,4096]{1,0:T(8,128)(2,1)} %param.5), dimensions={1,2} | broadcast | bytes 10485760 | tf_op jit(solution)/shard_map/stack | solution.py:13
  13.0 0.0 copy-start
  13.0 5.8 %all-to-all-start = ((bf16[4,256,4096]{2,1,0:T(8,128)(2,1)}), bf16[4,256,4096]{2,1,0:T(8,128)(2,1)}, u32[]{:S(2)}, u32[]{:S(2)}) async-start(bf16[4,256,4096]{2,1,0:T(8,128)(2,1)} %stack.2), calls=%async_computation | async-start | bytes 16777216 | tf_op jit(solution)/shard_map/all_to_all | solution.py:14
  18.8 0.0 reduce-scatter.3.cloned.1.call-start
  18.9 0.0 copy-done
  18.9 0.2 compare_reduce_fusion
  19.1 0.3 broadcast_in_dim.8
  19.4 2.4 reshape.81
  21.8 0.1 iota_add_fusion
  21.9 0.1 add.81
  22.0 90.9 %all-to-all-done = bf16[4,256,4096]{2,1,0:T(8,128)(2,1)} async-done(((bf16[4,256,4096]{2,1,0:T(8,128)(2,1)}), bf16[4,256,4096]{2,1,0:T(8,128)(2,1)}, u32[]{:S(2)}, u32[]{:S(2)}) %all-to-all-start) | async-done | bytes 8388640 | tf_op jit(solution)/shard_map/all_to_all | solution.py:14
  112.9 8.4 %select_reduce_fusion = (f32[512]{0:T(512)S(1)}, f32[512,1024]{1,0:T(8,128)S(1)}) fusion(pred[512,1024]{1,0:T(32,128)(4,1)S(1)} %reshape.81, bf16[512,4096]{1,0:T(8,128)(2,1)} %param.4, bf16[1024,4096]{1,0:T(8,128)(2,1)} %bitcast), kind=kOutput, calls=%fused_computation.4 | convolution fusion | flops 4296539648 | bytes 15206400 | tf_op jit(solution)/shard_map/dot_general | solution.py:18
  121.3 0.0 copy-start.1
  121.3 28.0 %pmax.7 = f32[512]{0:T(512)S(1)} all-reduce(f32[512]{0:T(512)S(1)} %get-tuple-element.2), channel_id=1, replica_groups=mesh['sect'=4,'pass'=16,'qry'=4] {'pass'}, use_global_device_ids=true, to_apply=%region_2.3 | all-reduce | flops 512 | bytes 4096 | tf_op jit(solution)/shard_map/pmax | solution.py:55
  149.3 0.7 fusion
  150.0 23.5 %psum.7 = f32[512]{0:T(512)S(1)} all-reduce(f32[512]{0:T(512)S(1)} %fusion), channel_id=1, replica_groups=mesh['sect'=4,'pass'=16,'qry'=4] {'pass'}, use_global_device_ids=true, to_apply=%region_4.5 | all-reduce | flops 512 | bytes 4096 | tf_op jit(solution)/shard_map/psum | solution.py:57
  173.6 0.0 copy-done.1
  173.6 10.3 %convolution_convert_fusion.1 = bf16[512,4096]{1,0:T(8,128)(2,1)} fusion(bf16[1024,4096]{1,0:T(8,128)(2,1)} %bitcast, pred[512,1024]{1,0:T(32,128)(4,1)S(1)} %reshape.81, f32[512,1024]{1,0:T(8,128)S(1)} %get-tuple-element.3, s32[1024]{0:T(1024)S(1)} %add.81, f32[512]{0:T(512)S(1)} %psum.7, f32[512]{0:T(512)S(1)} %pmax.7, s32[512]{0:T(512)S(1)} %copy-done.1), kind=kOutput, calls=%fused_computation.1 | convolution fusion | flops 4301783040 | bytes 15214592 | tf_op jit(solution)/shard_map/dot_general | solution.py:59
  183.8 0.0 reduce-scatter.3.cloned.1.call-update
  183.8 0.0 reduce-scatter.5.cloned.1.call-start
  183.9 9.5 %convolution_convert_fusion = bf16[1024,4096]{1,0:T(8,128)(2,1)} fusion(bf16[512,4096]{1,0:T(8,128)(2,1)} %param.4, pred[512,1024]{1,0:T(32,128)(4,1)S(1)} %reshape.81, f32[512,1024]{1,0:T(8,128)S(1)} %get-tuple-element.3, s32[1024]{0:T(1024)S(1)} %add.81, f32[512]{0:T(512)S(1)} %psum.7, f32[512]{0:T(512)S(1)} %pmax.7, s32[512]{0:T(512)S(1)} %copy-done.1), kind=kOutput, calls=%fused_computation | convolution fusion | flops 4303880192 | bytes 15214592 | tf_op jit(solution)/shard_map/dot_general | solution.py:24
  193.4 0.0 reduce-scatter.5.cloned.1.call-update
  193.4 50.3 %reduce-scatter.3.cloned.1.call-done = bf16[512,256]{1,0:T(8,128)(2,1)} async-done(((bf16[512,4096]{1,0:T(8,128)(2,1)}), bf16[512,256]{1,0:T(8,128)(2,1)}) %reduce-scatter.3.cloned.1.call-update) | async-done | bytes 262160 | tf_op jit(solution)/shard_map/reduce_scatter | solution.py:64
  243.8 93.6 %reduce-scatter.5.cloned.1.call-done = bf16[64,4096]{1,0:T(8,128)(2,1)} async-done(((bf16[1024,4096]{1,0:T(8,128)(2,1)}), bf16[64,4096]{1,0:T(8,128)(2,1)}) %reduce-scatter.5.cloned.1.call-update) | async-done | bytes 524304 | tf_op jit(solution)/shard_map/reduce_scatter | solution.py:69
  (1 shorter events, 0.0 us)
Async XLA Ops:
  13.0 5.9 %copy-start = (s32[2,64]{1,0:T(2,128)S(1)}, s32[2,64]{1,0:T(2,128)}, u32[]{:S(2)}) copy-start(s32[2,64]{1,0:T(2,128)} %param.6) | copy-start | bytes 1540
  13.0 99.9 %all-to-all-start = ((bf16[4,256,4096]{2,1,0:T(8,128)(2,1)}), bf16[4,256,4096]{2,1,0:T(8,128)(2,1)}, u32[]{:S(2)}, u32[]{:S(2)}) async-start(bf16[4,256,4096]{2,1,0:T(8,128)(2,1)} %stack.2), calls=%async_computation | async-start | bytes 16777216 | tf_op jit(solution)/shard_map/all_to_all | solution.py:14
  18.8 224.9 %reduce-scatter.3.cloned.1.call-start = ((), (), s32[]{:S(2)}) async-start(), calls=%async_computation.3 | async-start | bytes 4456448 | tf_op jit(solution)/shard_map/reduce_scatter | solution.py:64
  121.3 52.2 %copy-start.1 = (s32[512]{0:T(512)S(1)}, s32[512]{0:T(512)}, u32[]{:S(2)}) copy-start(s32[512]{0:T(512)} %param.7) | copy-start | bytes 6148
  183.8 153.5 %reduce-scatter.5.cloned.1.call-start = ((), (), s32[]{:S(2)}) async-start(), calls=%async_computation.4 | async-start | bytes 8912896 | tf_op jit(solution)/shard_map/reduce_scatter | solution.py:69
Sparse Core Ops, SparseCore 0:
  184.0 59.7 reduce-scatter.2
  248.0 89.2 reduce-scatter.4
